TPU v7x, 32 devices: a whole 2x2x4 slice. The times are simulated.
32 devices in a mesh: dp: 16 (over z, y, x), aug: 2 (over core).
Axes of the slice: x: 2, y: 2, z: 4, core: 2. Of those that a mesh axis runs over, the one named last changes fastest.
Arguments:
- images: bfloat16 [2, 16, 197, 768], P('aug', 'dp'), may hold values from -6 to 6
- out_grads: bfloat16 [2, 16, 197, 768], P('aug', 'dp'), may hold values from -8 to 8
- up_weight_t: bfloat16 [3072, 768], P(('dp', 'aug')), may hold values from -0.21875 to 0.21875
- down_weight_t: bfloat16 [3072, 768], P(('dp', 'aug')), may hold values from -0.21875 to 0.21875
- left_up: bfloat16 [3072, 128], P(('dp', 'aug')), may hold values from -0.109375 to 0.109375
- right_up: bfloat16 [768, 128], replicated, may hold values from -0.21875 to 0.21875
- left_down: bfloat16 [768, 128], replicated, may hold values from -0.21875 to 0.21875
- right_down: bfloat16 [3072, 128], P(('dp', 'aug')), may hold values from -0.109375 to 0.109375
- noise: float32 [2, 128, 128], P(None, 'aug'), may hold values from -6 to 6
Outputs:
- update: float32 [2, 128, 128], P(None, 'aug')
- clip_scales: float32 [16], P('dp')
All inputs are finite; a program needn't handle non-finite values.
Results may differ from a plain program's by a relative error of at most 0.0032.
Values may be sent and summed in bfloat16 or wider, within the bound.
A program may use at most 64 MiB of HBM per device.

v0:
```python
import math
import jax
import jax.numpy as jnp
from jax import lax
from jax.sharding import PartitionSpec as P

gelu_coef = 0.7978845608028654
clip_frac = 0.3
noise_mult = 0.05


def gelu_pair(hidden):
    inner = gelu_coef * (hidden + 0.044715 * hidden * hidden * hidden)
    tangent = jnp.tanh(inner)
    value = 0.5 * hidden * (1.0 + tangent)
    slope = 0.5 * (1.0 + tangent) + 0.5 * hidden * (1.0 - tangent * tangent) * gelu_coef * (
        1.0 + 3.0 * 0.044715 * hidden * hidden
    )
    return (value, slope)


def contract_last(left, right):
    return lax.dot_general(
        left, right, (((1,), (1,)), ((), ())), preferred_element_type=jnp.float32
    )


def local(
    images, out_grads, up_weight_t, down_weight_t, left_up, right_up, left_down, right_down, noise
):
    local_augs = images.shape[0]
    local_images = images.shape[1]
    tokens = images.shape[2]
    width = images.shape[3]
    rank = right_up.shape[1]
    token_rows = images.reshape(-1, width)
    grad_rows = out_grads.reshape(-1, width)
    up_piece = lax.all_gather(up_weight_t, ("dp", "aug"), axis=0, tiled=True)
    down_piece = lax.all_gather(down_weight_t, ("dp", "aug"), axis=0, tiled=True)
    left_piece = lax.all_gather(left_up, ("dp", "aug"), axis=0, tiled=True)
    right_piece = lax.all_gather(right_down, ("dp", "aug"), axis=0, tiled=True)
    hidden = contract_last(token_rows, up_piece)
    activation, slope = gelu_pair(hidden)
    back = contract_last(grad_rows, down_piece)
    hidden_grad = (back * slope).astype(jnp.bfloat16)
    first = jnp.dot(hidden_grad, left_piece, preferred_element_type=jnp.float32)
    second = jnp.dot(
        activation.astype(jnp.bfloat16), right_piece, preferred_element_type=jnp.float32
    )
    up_total = first
    down_total = second
    v_up = up_total.astype(jnp.bfloat16)
    u_down = down_total.astype(jnp.bfloat16)
    u_up = jnp.dot(token_rows, right_up, preferred_element_type=jnp.float32).astype(jnp.bfloat16)
    v_down = jnp.dot(grad_rows, left_down, preferred_element_type=jnp.float32).astype(jnp.bfloat16)
    shape = (local_augs, local_images, tokens, rank)
    first = jnp.einsum(
        "aitr,aits->irs",
        v_up.reshape(shape),
        u_up.reshape(shape),
        preferred_element_type=jnp.float32,
    )
    second = jnp.einsum(
        "aitr,aits->irs",
        v_down.reshape(shape),
        u_down.reshape(shape),
        preferred_element_type=jnp.float32,
    )
    local_terms = jnp.stack([first, second], axis=1)
    all_augs = local_augs * lax.axis_size("aug")
    row_sums = lax.psum_scatter(local_terms, "aug", scatter_dimension=2, tiled=True)
    my_rows = row_sums / all_augs
    squares = lax.psum(jnp.sum(my_rows * my_rows, axis=(1, 2, 3)), "aug")
    norms = jnp.sqrt(squares + 1e-06)
    clip_norm = clip_frac * rank * math.sqrt(tokens / all_augs)
    clip_scales = jnp.minimum(1.0, clip_norm / norms)
    clipped_rows = jnp.sum(clip_scales[:, None, None, None] * my_rows, axis=0)
    summed_rows = lax.psum(clipped_rows, "dp")
    all_images = local_images * lax.axis_size("dp")
    update = (summed_rows + noise_mult * clip_norm * noise) / jnp.sqrt(jnp.float32(all_images))
    return (update, clip_scales)


def solution(mesh):
    placed = (
        P("aug", "dp", None, None),
        P("aug", "dp", None, None),
        P(("dp", "aug"), None),
        P(("dp", "aug"), None),
        P(("dp", "aug"), None),
        P(),
        P(),
        P(("dp", "aug"), None),
        P(None, "aug", None),
    )
    return jax.shard_map(
        local,
        mesh=mesh,
        in_specs=placed,
        out_specs=(P(None, "aug", None), P("dp")),
        check_vma=False,
    )
```

profile of v0, /device:TPU:0, one launch (start us, length us, event | category | flops | bytes accessed | tf_op | source)
XLA Modules:
  0.0 281.8 jit_solution(15459410550856716134)
XLA Ops:
  7.2 0.0 copy-start
  7.2 0.0 all-gather.5.cloned.1.call-start
  7.2 0.7 all-gather.5.cloned.1.call-update
  7.9 0.0 all-gather.3.cloned.1.call-start
  8.0 0.7 all-gather.3.cloned.1.call-update
  8.7 0.0 reduce-scatter.2.cloned.1.call-start
  8.7 46.2 %all_gather.14 = bf16[3072,128]{1,0:T(8,128)(2,1)S(1)} all-gather(bf16[96,128]{1,0:T(8,128)(2,1)} %param.13), channel_id=1, replica_groups=mesh['dp'=16,'aug'=2] {'dp','aug'}, dimensions={0}, use_global_device_ids=true | all-gather | bytes 811008 | tf_op jit(solution)/shard_map/all_gather | solution.py:40
  54.9 42.6 %all_gather.15 = bf16[3072,128]{1,0:T(8,128)(2,1)} all-gather(bf16[96,128]{1,0:T(8,128)(2,1)} %param.16), channel_id=1, replica_groups=mesh['dp'=16,'aug'=2] {'dp','aug'}, dimensions={0}, use_global_device_ids=true | all-gather | bytes 811008 | tf_op jit(solution)/shard_map/all_gather | solution.py:41
  97.5 0.0 all-gather.5.cloned.1.call-done
  97.5 0.0 copy-done
  97.5 0.0 copy-start.1
  97.5 4.0 %fusion.17 = f32[197,3072]{1,0:T(8,128)S(1)} fusion(bf16[3072,768]{1,0:T(8,128)(2,1)} %all-gather.5.cloned.1.call-done, bf16[1,1,197,768]{3,2,1,0:T(8,128)(2,1)S(1)} %copy-done), kind=kOutput, calls=%fused_computation.24 | convolution fusion | flops 929562624 | bytes 7441920 | tf_op jit(solution)/shard_map/dot_general | solution.py:23
  101.5 0.0 copy-done.1
  101.5 1.6 fusion.14
  103.1 42.8 %all-gather.3.cloned.1.call-done = bf16[3072,768]{1,0:T(8,128)(2,1)} async-done(((bf16[96,768]{1,0:T(8,128)(2,1)}), bf16[3072,768]{1,0:T(8,128)(2,1)}) %all-gather.3.cloned.1.call-update) | async-done | bytes 4718608 | tf_op jit(solution)/shard_map/all_gather | solution.py:39
  145.9 5.6 %fusion.13 = bf16[197,128]{1,0:T(8,128)(2,1)} fusion(bf16[3072,128]{1,0:T(8,128)(2,1)S(1)} %all_gather.14, bf16[3072,768]{1,0:T(8,128)(2,1)} %all-gather.3.cloned.1.call-done, f32[197,3072]{1,0:T(8,128)S(1)} %fusion.17, bf16[1,1,197,768]{3,2,1,0:T(8,128)(2,1)} %param.10), kind=kOutput, calls=%fused_computation.17 | convolution fusion | flops 1096013440 | bytes 8278784 | tf_op jit(solution)/shard_map/dot_general | solution.py:46
  151.5 1.4 convolution_bitcast_fusion.1
  152.9 1.5 convolution_bitcast_fusion
  154.4 0.7 pad_maximum_fusion
  155.1 0.0 reduce-scatter.2.cloned.1.call-update
  155.1 0.0 all-reduce.2.cloned.1.call-start
  155.1 6.0 %reduce-scatter.2.cloned.1.call-done = f32[1,2,64,128]{3,2,1,0:T(8,128)} async-done(((f32[1,2,128,128]{3,2,1,0:T(8,128)}), f32[1,2,64,128]{3,2,1,0:T(8,128)}) %reduce-scatter.2.cloned.1.call-update) | async-done | bytes 65552 | tf_op jit(solution)/shard_map/reduce_scatter | solution.py:71
  161.1 1.5 multiply_reduce_fusion
  162.6 3.1 %psum.14 = f32[1]{0:T(128)} all-reduce(f32[1]{0:T(128)} %bitcast.4), channel_id=1, replica_groups=mesh['dp'=16,'aug'=2] {'aug'}, use_global_device_ids=true, to_apply=%region_2.0 | all-reduce | flops 1 | bytes 8 | tf_op jit(solution)/shard_map/psum | solution.py:73
  166.4 1.5 multiply_bitcast_fusion
  167.8 0.0 all-reduce.2.cloned.1.call-update
  167.9 104.8 %all-reduce.2.cloned.1.call-done = f32[2,64,128]{2,1,0:T(8,128)} async-done(((f32[2,64,128]{2,1,0:T(8,128)}), f32[2,64,128]{2,1,0:T(8,128)}) %all-reduce.2.cloned.1.call-update) | async-done | bytes 65552 | tf_op jit(solution)/shard_map/psum | solution.py:78
  272.6 1.5 add_multiply_fusion
Async XLA Ops:
  7.2 90.3 %copy-start = (bf16[1,1,197,768]{3,2,1,0:T(8,128)(2,1)S(1)}, bf16[1,1,197,768]{3,2,1,0:T(8,128)(2,1)}, u32[]{:S(2)}) copy-start(bf16[1,1,197,768]{3,2,1,0:T(8,128)(2,1)} %param.9) | copy-start | bytes 907780
  7.2 90.3 %all-gather.5.cloned.1.call-start = ((), (), s32[]{:S(2)}) async-start(), calls=%async_computation.2 | async-start | bytes 4866048 | tf_op jit(solution)/shard_map/all_gather | solution.py:38
  7.9 138.0 %all-gather.3.cloned.1.call-start = ((), (), s32[]{:S(2)}) async-start(), calls=%async_computation.1 | async-start | bytes 4866048 | tf_op jit(solution)/shard_map/all_gather | solution.py:39
  8.7 152.5 %reduce-scatter.2.cloned.1.call-start = ((), (), s32[]{:S(2)}) async-start(), calls=%async_computation.3 | async-start | bytes 196608 | tf_op jit(solution)/shard_map/reduce_scatter | solution.py:71
  97.5 4.0 %copy-start.1 = (bf16[3072,128]{1,0:T(8,128)(2,1)S(1)}, bf16[3072,128]{1,0:T(8,128)(2,1)}, u32[]{:S(2)}) copy-start(bf16[3072,128]{1,0:T(8,128)(2,1)} %all_gather.15) | copy-start | bytes 2359300
  155.1 117.5 %all-reduce.2.cloned.1.call-start = ((), (), s32[]{:S(2)}) async-start(), calls=%async_computation.4 | async-start | bytes 131072 | tf_op jit(solution)/shard_map/psum | solution.py:78
Sparse Core Ops, SparseCore 0:
  10.9 69.5 all-gather.4
  83.4 62.4 all-gather.2
  155.2 5.8 reduce-scatter.1
  168.0 104.5 all-reduce.1
where the time goes:
time: 282 us
  waiting for transfers between devices  155 us (55%)
  blocking collectives  91.9 us (33%)
  between operations  15.6 us (6%)
  matrix products  14.1 us (5%)
  other arithmetic  5.11 us (2%)
    psum x1, waiting for transfers between devices, local(): summed_rows = lax.psum(clipped_rows, 'dp')  105 us
    all_gather x1, blocking collectives, local(): left_piece = lax.all_gather(left_up, ('dp', 'aug'), axis=0, tiled=True)  46.2 us
    all_gather x1, waiting for transfers between devices, local(): lax.all_gather(down_weight_t, ('dp', 'aug'), axis=0, tiled=True)  42.8 us
    all_gather x1, blocking collectives, local(): right_piece = lax.all_gather(right_down, ('dp', 'aug'), axis=0, tiled=True)  42.6 us
    reduce_scatter x1, waiting for transfers between devices, local(): lax.psum_scatter(local_terms, 'aug', scatter_dimension=2, tiled=True)  5.99 us
  transfers between devices with their start and end apart: 4, of which 3 were waited for; matrix products, arithmetic and copies ran while one was open for 2% of the time, Pallas kernels for 0%

commit v1 on v0

--- a/solution.py
+++ b/solution.py
@@ -36,8 +36,13 @@
     token_rows = images.reshape(-1, width)
     grad_rows = out_grads.reshape(-1, width)
     up_piece = lax.all_gather(up_weight_t, ("dp", "aug"), axis=0, tiled=True)
-    down_piece = lax.all_gather(down_weight_t, ("dp", "aug"), axis=0, tiled=True)
-    left_piece = lax.all_gather(left_up, ("dp", "aug"), axis=0, tiled=True)
+    down_piece, left_piece = jnp.split(
+        lax.all_gather(
+            jnp.concatenate([down_weight_t, left_up], axis=1), ("dp", "aug"), axis=0, tiled=True
+        ),
+        [down_weight_t.shape[1]],
+        axis=1,
+    )
     right_piece = lax.all_gather(right_down, ("dp", "aug"), axis=0, tiled=True)
     hidden = contract_last(token_rows, up_piece)
     activation, slope = gelu_pair(hidden)

time: 282 us -> 279 us (0.989)
  blocking collectives: 91.9 us -> 49.6 us
  waiting for transfers between devices: 155 us -> 194 us
    all_gather x1 -> x0, blocking collectives: 46.2 us -> none  [local(): left_piece = lax.all_gather(left_up, ('dp', 'aug'), axis=0, tiled=True)]
    all_gather x1, waiting for transfers between devices: 0.01 us -> 22 us  [local(): up_piece = lax.all_gather(up_weight_t, ('dp', 'aug'), axis=0, tiled=True)]
    all_gather x1, waiting for transfers between devices: 42.8 us -> 60.4 us  [local(): lax.all_gather(jnp.concatenate([down_weight_t, left_up], axis=1), ('dp',...]
    all_gather x1, blocking collectives: 42.6 us -> 46.5 us  [local(): right_piece = lax.all_gather(right_down, ('dp', 'aug'), axis=0, tiled=True)]
  transfers between devices with their start and end apart: 4 -> 4, of which waited for: 3 -> 4; matrix products, arithmetic and copies ran while one was open for 2% -> 3% of each run, Pallas kernels for 0% -> 0%
where the time goes in v1:
time: 279 us
  waiting for transfers between devices  194 us (70%)
  blocking collectives  49.6 us (18%)
  between operations  15.6 us (6%)
  matrix products  12.8 us (5%)
  other arithmetic  6.69 us (2%)
    psum x1, waiting for transfers between devices, local(): summed_rows = lax.psum(clipped_rows, 'dp')  105 us
    all_gather x1, waiting for transfers between devices, local(): lax.all_gather(jnp.concatenate([down_weight_t, left_up], axis=1), ('dp',...  60.4 us
    all_gather x1, blocking collectives, local(): right_piece = lax.all_gather(right_down, ('dp', 'aug'), axis=0, tiled=True)  46.5 us
    all_gather x1, waiting for transfers between devices, local(): up_piece = lax.all_gather(up_weight_t, ('dp', 'aug'), axis=0, tiled=True)  22 us
    reduce_scatter x1, waiting for transfers between devices, local(): lax.psum_scatter(local_terms, 'aug', scatter_dimension=2, tiled=True)  6.38 us
  transfers between devices with their start and end apart: 4, of which 4 were waited for; matrix products, arithmetic and copies ran while one was open for 3% of the time, Pallas kernels for 0%

profile of v1, /device:TPU:0, one launch (start us, length us, event | category | flops | bytes accessed | tf_op | source)
XLA Modules:
  0.0 279.1 jit_solution(5197794020085837020)
XLA Ops:
  7.2 0.0 copy-start
  7.2 0.0 all-gather.5.cloned.1.call-start
  7.2 0.7 all-gather.5.cloned.1.call-update
  7.9 0.0 all-gather.3.cloned.1.call-start
  8.0 1.6 pad_maximum_fusion
  9.6 0.0 all-gather.3.cloned.1.call-update
  9.6 0.0 reduce-scatter.2.cloned.1.call-start
  9.6 46.5 %all_gather.11 = bf16[3072,128]{1,0:T(8,128)(2,1)S(1)} all-gather(bf16[96,128]{1,0:T(8,128)(2,1)} %param.16), channel_id=1, replica_groups=mesh['dp'=16,'aug'=2] {'dp','aug'}, dimensions={0}, use_global_device_ids=true | all-gather | bytes 811008 | tf_op jit(solution)/shard_map/all_gather | solution.py:46
  56.1 22.0 %all-gather.5.cloned.1.call-done = bf16[3072,768]{1,0:T(8,128)(2,1)} async-done(((bf16[96,768]{1,0:T(8,128)(2,1)}), bf16[3072,768]{1,0:T(8,128)(2,1)}) %all-gather.5.cloned.1.call-update) | async-done | bytes 4718608 | tf_op jit(solution)/shard_map/all_gather | solution.py:38
  78.1 0.0 copy-done
  78.1 3.9 %fusion.32 = f32[197,3072]{1,0:T(8,128)S(1)} fusion(bf16[3072,768]{1,0:T(8,128)(2,1)} %all-gather.5.cloned.1.call-done, bf16[1,1,197,768]{3,2,1,0:T(8,128)(2,1)S(1)} %copy-done), kind=kOutput, calls=%fused_computation.28 | convolution fusion | flops 929562624 | bytes 7441920 | tf_op jit(solution)/shard_map/dot_general | solution.py:23
  82.1 1.6 fusion.28
  83.7 1.5 convolution_bitcast_fusion
  85.2 0.0 copy-start.1
  85.2 0.0 copy-start.2
  85.2 60.4 %all-gather.3.cloned.1.call-done = bf16[3072,896]{1,0:T(8,128)(2,1)} async-done(((bf16[96,896]{1,0:T(8,128)(2,1)}), bf16[3072,896]{1,0:T(8,128)(2,1)}) %all-gather.3.cloned.1.call-update) | async-done | bytes 5505040 | tf_op jit(solution)/shard_map/all_gather | solution.py:40
  145.6 5.3 %fusion.25 = bf16[197,128]{1,0:T(8,128)(2,1)S(1)} fusion(bf16[3072,896]{1,0:T(8,128)(2,1)} %all-gather.3.cloned.1.call-done, f32[197,3072]{1,0:T(8,128)S(1)} %fusion.32, bf16[1,1,197,768]{3,2,1,0:T(8,128)(2,1)} %param.10), kind=kOutput, calls=%fused_computation.20 | convolution fusion | flops 1096013440 | bytes 8278784 | tf_op jit(solution)/shard_map/dot_general | solution.py:51
  150.9 0.0 copy-done.1
  150.9 0.4 convolution_bitcast_fusion.1
  151.3 0.7 pad_maximum_fusion.1
  152.0 0.0 reduce-scatter.2.cloned.1.call-update
  152.0 0.0 all-reduce.2.cloned.1.call-start
  152.1 6.4 %reduce-scatter.2.cloned.1.call-done = f32[1,2,64,128]{3,2,1,0:T(8,128)} async-done(((f32[1,2,128,128]{3,2,1,0:T(8,128)}), f32[1,2,64,128]{3,2,1,0:T(8,128)}) %reduce-scatter.2.cloned.1.call-update) | async-done | bytes 65552 | tf_op jit(solution)/shard_map/reduce_scatter | solution.py:76
  158.4 1.5 multiply_reduce_fusion
  159.9 3.1 %psum.14 = f32[1]{0:T(128)} all-reduce(f32[1]{0:T(128)} %bitcast.5), channel_id=1, replica_groups=mesh['dp'=16,'aug'=2] {'aug'}, use_global_device_ids=true, to_apply=%region_2.0 | all-reduce | flops 1 | bytes 8 | tf_op jit(solution)/shard_map/psum | solution.py:78
  163.7 1.5 multiply_bitcast_fusion
  165.2 0.0 all-reduce.2.cloned.1.call-update
  165.2 104.8 %all-reduce.2.cloned.1.call-done = f32[2,64,128]{2,1,0:T(8,128)} async-done(((f32[2,64,128]{2,1,0:T(8,128)}), f32[2,64,128]{2,1,0:T(8,128)}) %all-reduce.2.cloned.1.call-update) | async-done | bytes 65552 | tf_op jit(solution)/shard_map/psum | solution.py:83
  270.0 0.0 copy-done.2
  270.0 1.5 add_multiply_fusion
Async XLA Ops:
  7.2 71.0 %copy-start = (bf16[1,1,197,768]{3,2,1,0:T(8,128)(2,1)S(1)}, bf16[1,1,197,768]{3,2,1,0:T(8,128)(2,1)}, u32[]{:S(2)}) copy-start(bf16[1,1,197,768]{3,2,1,0:T(8,128)(2,1)} %param.9) | copy-start | bytes 907780
  7.2 70.9 %all-gather.5.cloned.1.call-start = ((), (), s32[]{:S(2)}) async-start(), calls=%async_computation.2 | async-start | bytes 4866048 | tf_op jit(solution)/shard_map/all_gather | solution.py:38
  7.9 137.7 %all-gather.3.cloned.1.call-start = ((), (), s32[]{:S(2)}) async-start(), calls=%async_computation.1 | async-start | bytes 5677056 | tf_op jit(solution)/shard_map/all_gather | solution.py:40
  9.6 148.8 %reduce-scatter.2.cloned.1.call-start = ((), (), s32[]{:S(2)}) async-start(), calls=%async_computation.3 | async-start | bytes 196608 | tf_op jit(solution)/shard_map/reduce_scatter | solution.py:76
  85.2 65.7 %copy-start.1 = (bf16[768,128]{1,0:T(8,128)(2,1)S(1)}, bf16[768,128]{1,0:T(8,128)(2,1)}, u32[]{:S(2)}) copy-start(bf16[768,128]{1,0:T(8,128)(2,1)} %param.14) | copy-start | bytes 589828
  85.2 184.7 %copy-start.2 = (f32[2,64,128]{2,1,0:T(8,128)S(1)}, f32[2,64,128]{2,1,0:T(8,128)}, u32[]{:S(2)}) copy-start(f32[2,64,128]{2,1,0:T(8,128)} %param.17) | copy-start | bytes 196612
  152.0 117.9 %all-reduce.2.cloned.1.call-start = ((), (), s32[]{:S(2)}) async-start(), calls=%async_computation.4 | async-start | bytes 131072 | tf_op jit(solution)/shard_map/psum | solution.py:83
Sparse Core Ops, SparseCore 0:
  10.9 67.1 all-gather.4
  81.0 64.5 all-gather.2
  152.1 6.2 reduce-scatter.1
  165.3 104.6 all-reduce.1

commit v2 on v0

--- a/solution.py
+++ b/solution.py
@@ -75,7 +75,7 @@
     clip_norm = clip_frac * rank * math.sqrt(tokens / all_augs)
     clip_scales = jnp.minimum(1.0, clip_norm / norms)
     clipped_rows = jnp.sum(clip_scales[:, None, None, None] * my_rows, axis=0)
-    summed_rows = lax.psum(clipped_rows, "dp")
+    summed_rows = jnp.sum(lax.all_gather(clipped_rows, "dp"), axis=0)
     all_images = local_images * lax.axis_size("dp")
     update = (summed_rows + noise_mult * clip_norm * noise) / jnp.sqrt(jnp.float32(all_images))
     return (update, clip_scales)

time: 282 us -> 234 us (0.83)
  waiting for transfers between devices: 155 us -> 107 us
    psum x1 -> x0, waiting for transfers between devices: 105 us -> none  [local(): summed_rows = lax.psum(clipped_rows, 'dp')]
    all_gather x0 -> x1, waiting for transfers between devices: none -> 56.4 us  [local(): summed_rows = jnp.sum(lax.all_gather(clipped_rows, 'dp'), axis=0)]
where the time goes in v2:
time: 234 us
  waiting for transfers between devices  107 us (46%)
  blocking collectives  91.9 us (39%)
  between operations  15.6 us (7%)
  matrix products  14.2 us (6%)
  other arithmetic  5.53 us (2%)
    all_gather x1, waiting for transfers between devices, local(): summed_rows = jnp.sum(lax.all_gather(clipped_rows, 'dp'), axis=0)  56.4 us
    all_gather x1, blocking collectives, local(): left_piece = lax.all_gather(left_up, ('dp', 'aug'), axis=0, tiled=True)  46.2 us
    all_gather x1, waiting for transfers between devices, local(): lax.all_gather(down_weight_t, ('dp', 'aug'), axis=0, tiled=True)  42.8 us
    all_gather x1, blocking collectives, local(): right_piece = lax.all_gather(right_down, ('dp', 'aug'), axis=0, tiled=True)  42.6 us
    reduce_scatter x1, waiting for transfers between devices, local(): lax.psum_scatter(local_terms, 'aug', scatter_dimension=2, tiled=True)  5.99 us
    dot_general x1, matrix products, local(): first = jnp.dot(hidden_grad, left_piece, preferred_element_type=jnp.float32)  5.61 us
  transfers between devices with their start and end apart: 4, of which 3 were waited for; matrix products, arithmetic and copies ran while one was open for 2% of the time, Pallas kernels for 0%

profile of v2, /device:TPU:0, one launch (start us, length us, event | category | flops | bytes accessed | tf_op | source)
XLA Modules:
  0.0 233.9 jit_solution(16129593150368034898)
XLA Ops:
  7.2 0.0 copy-start
  7.2 0.0 all-gather.6.cloned.1.call-start
  7.2 0.7 all-gather.6.cloned.1.call-update
  7.9 0.0 all-gather.4.cloned.1.call-start
  8.0 0.7 all-gather.4.cloned.1.call-update
  8.7 0.0 reduce-scatter.2.cloned.1.call-start
  8.7 46.2 %all_gather.18 = bf16[3072,128]{1,0:T(8,128)(2,1)S(1)} all-gather(bf16[96,128]{1,0:T(8,128)(2,1)} %param.13), channel_id=1, replica_groups=mesh['dp'=16,'aug'=2] {'dp','aug'}, dimensions={0}, use_global_device_ids=true | all-gather | bytes 811008 | tf_op jit(solution)/shard_map/all_gather | solution.py:40
  54.9 42.6 %all_gather.19 = bf16[3072,128]{1,0:T(8,128)(2,1)} all-gather(bf16[96,128]{1,0:T(8,128)(2,1)} %param.16), channel_id=1, replica_groups=mesh['dp'=16,'aug'=2] {'dp','aug'}, dimensions={0}, use_global_device_ids=true | all-gather | bytes 811008 | tf_op jit(solution)/shard_map/all_gather | solution.py:41
  97.5 0.0 all-gather.6.cloned.1.call-done
  97.5 0.0 copy-done
  97.5 0.0 copy-start.1
  97.5 4.0 %fusion.17 = f32[197,3072]{1,0:T(8,128)S(1)} fusion(bf16[3072,768]{1,0:T(8,128)(2,1)} %all-gather.6.cloned.1.call-done, bf16[1,1,197,768]{3,2,1,0:T(8,128)(2,1)S(1)} %copy-done), kind=kOutput, calls=%fused_computation.24 | convolution fusion | flops 929562624 | bytes 7441920 | tf_op jit(solution)/shard_map/dot_general | solution.py:23
  101.5 0.0 copy-done.1
  101.5 1.6 fusion.14
  103.1 42.8 %all-gather.4.cloned.1.call-done = bf16[3072,768]{1,0:T(8,128)(2,1)} async-done(((bf16[96,768]{1,0:T(8,128)(2,1)}), bf16[3072,768]{1,0:T(8,128)(2,1)}) %all-gather.4.cloned.1.call-update) | async-done | bytes 4718608 | tf_op jit(solution)/shard_map/all_gather | solution.py:39
  145.9 5.6 %fusion.13 = bf16[197,128]{1,0:T(8,128)(2,1)} fusion(bf16[3072,128]{1,0:T(8,128)(2,1)S(1)} %all_gather.18, bf16[3072,768]{1,0:T(8,128)(2,1)} %all-gather.4.cloned.1.call-done, f32[197,3072]{1,0:T(8,128)S(1)} %fusion.17, bf16[1,1,197,768]{3,2,1,0:T(8,128)(2,1)} %param.10), kind=kOutput, calls=%fused_computation.17 | convolution fusion | flops 1096013440 | bytes 8278784 | tf_op jit(solution)/shard_map/dot_general | solution.py:46
  151.5 0.0 copy-start.2
  151.5 1.4 convolution_bitcast_fusion.1
  152.9 1.5 convolution_bitcast_fusion
  154.4 0.7 pad_maximum_fusion
  155.1 0.0 reduce-scatter.2.cloned.1.call-update
  155.1 0.0 all-gather.8.cloned.1.call-start
  155.2 6.0 %reduce-scatter.2.cloned.1.call-done = f32[1,2,64,128]{3,2,1,0:T(8,128)} async-done(((f32[1,2,128,128]{3,2,1,0:T(8,128)}), f32[1,2,64,128]{3,2,1,0:T(8,128)}) %reduce-scatter.2.cloned.1.call-update) | async-done | bytes 65552 | tf_op jit(solution)/shard_map/reduce_scatter | solution.py:71
  161.2 1.5 multiply_reduce_fusion
  162.6 3.1 %psum.7 = f32[1]{0:T(128)} all-reduce(f32[1]{0:T(128)} %bitcast.4), channel_id=1, replica_groups=mesh['dp'=16,'aug'=2] {'aug'}, use_global_device_ids=true, to_apply=%region_2.0 | all-reduce | flops 1 | bytes 8 | tf_op jit(solution)/shard_map/psum | solution.py:73
  166.4 1.5 broadcast_multiply_fusion
  167.9 0.0 all-gather.8.cloned.1.call-update
  167.9 56.4 %all-gather.8.cloned.1.call-done = f32[16,2,64,128]{3,2,1,0:T(8,128)} async-done(((f32[1,2,64,128]{3,2,1,0:T(8,128)}), f32[16,2,64,128]{3,2,1,0:T(8,128)}) %all-gather.8.cloned.1.call-update) | async-done | bytes 1048592 | tf_op jit(solution)/shard_map/all_gather | solution.py:78
  224.3 1.3 reduce_sum.26
  225.6 0.0 copy-done.2
  225.6 0.6 add_multiply_fusion
Async XLA Ops:
  7.2 90.3 %copy-start = (bf16[1,1,197,768]{3,2,1,0:T(8,128)(2,1)S(1)}, bf16[1,1,197,768]{3,2,1,0:T(8,128)(2,1)}, u32[]{:S(2)}) copy-start(bf16[1,1,197,768]{3,2,1,0:T(8,128)(2,1)} %param.9) | copy-start | bytes 907780
  7.2 90.3 %all-gather.6.cloned.1.call-start = ((), (), s32[]{:S(2)}) async-start(), calls=%async_computation.2 | async-start | bytes 4866048 | tf_op jit(solution)/shard_map/all_gather | solution.py:38
  7.9 138.0 %all-gather.4.cloned.1.call-start = ((), (), s32[]{:S(2)}) async-start(), calls=%async_computation.1 | async-start | bytes 4866048 | tf_op jit(solution)/shard_map/all_gather | solution.py:39
  8.7 152.5 %reduce-scatter.2.cloned.1.call-start = ((), (), s32[]{:S(2)}) async-start(), calls=%async_computation.3 | async-start | bytes 196608 | tf_op jit(solution)/shard_map/reduce_scatter | solution.py:71
  97.5 4.0 %copy-start.1 = (bf16[3072,128]{1,0:T(8,128)(2,1)S(1)}, bf16[3072,128]{1,0:T(8,128)(2,1)}, u32[]{:S(2)}) copy-start(bf16[3072,128]{1,0:T(8,128)(2,1)} %all_gather.19) | copy-start | bytes 2359300
  151.5 74.1 %copy-start.2 = (f32[2,64,128]{2,1,0:T(8,128)S(1)}, f32[2,64,128]{2,1,0:T(8,128)}, u32[]{:S(2)}) copy-start(f32[2,64,128]{2,1,0:T(8,128)} %param.17) | copy-start | bytes 196612
  155.1 69.1 %all-gather.8.cloned.1.call-start = ((), (), s32[]{:S(2)}) async-start(), calls=%async_computation.4 | async-start | bytes 1114112 | tf_op jit(solution)/shard_map/all_gather | solution.py:78
Sparse Core Ops, SparseCore 0:
  10.9 69.5 all-gather.5
  83.4 62.4 all-gather.3
  155.3 5.8 reduce-scatter.1
  168.0 56.2 all-gather.7
